TPU v7x, 32 devices: a whole 2x2x4 slice. The times are simulated.
32 devices in a mesh: stream: 2 (over core), dp: 16 (over z, y, x).
Axes of the slice: x: 2, y: 2, z: 4, core: 2. Of those that a mesh axis runs over, the one named last changes fastest.
Arguments:
- layer_input: bfloat16 [2, 16384, 768], P('stream', 'dp'), may hold values from -6 to 6
- pair_group: int32 [256], P('dp'), may hold values from 0 to 108, as said below
- query_weight: bfloat16 [768, 768], replicated, may hold values from -0.21875 to 0.21875
- query_bias: float32 [768], replicated, may hold values from -4 to 4
- key_weight: bfloat16 [768, 768], replicated, may hold values from -0.21875 to 0.21875
- value_weight: bfloat16 [768, 768], replicated, may hold values from -0.21875 to 0.21875
- value_bias: float32 [768], replicated, may hold values from -4 to 4
- out_weight: bfloat16 [768, 768], replicated, may hold values from -1 to 1
- out_bias: float32 [768], replicated, may hold values from -4 to 4
- mixer_gain: float32 [768], replicated, may hold values from 0.1 to 1.9
- mixer_shift: float32 [768], replicated, may hold values from -4 to 4
- up_weight: bfloat16 [768, 3072], replicated, may hold values from -0.21875 to 0.21875
- up_bias: float32 [3072], replicated, may hold values from -4 to 4
- down_weight: bfloat16 [3072, 768], replicated, may hold values from -0.109375 to 0.109375
- down_bias: float32 [768], replicated, may hold values from -4 to 4
- final_gain: float32 [768], replicated, may hold values from 0.1 to 1.9
- final_shift: float32 [768], replicated, may hold values from -4 to 4
- upstream: bfloat16 [2, 16384, 768], P('stream', 'dp'), may hold values from -0.75 to 0.75
Outputs:
- layer_output: bfloat16 [2, 16384, 768], P('stream', 'dp')
- input_grad: float32 [2, 16384, 768], P('stream', 'dp')
- total_loss: float32 [2, 256], P('stream', 'dp')
- query_weight_grad: float32 [768, 768], replicated
- query_bias_grad: float32 [768], replicated
- key_weight_grad: float32 [768, 768], replicated
- value_weight_grad: float32 [768, 768], replicated
- value_bias_grad: float32 [768], replicated
- out_weight_grad: float32 [768, 768], replicated
- out_bias_grad: float32 [768], replicated
- mixer_gain_grad: float32 [768], replicated
- mixer_shift_grad: float32 [768], replicated
- up_weight_grad: float32 [768, 3072], replicated
- up_bias_grad: float32 [3072], replicated
- down_weight_grad: float32 [3072, 768], replicated
- down_bias_grad: float32 [768], replicated
- final_gain_grad: float32 [768], replicated
- final_shift_grad: float32 [768], replicated
Inputs may be any that keep to these rules, and one draw needn't show every extreme that they name: `pair_group`: every one of the 109 ids names 2 or more pairs; the first and the last pair have the same id.
All inputs are finite; a program needn't handle non-finite values.
Results may differ from a plain program's by a relative error of at most 0.014.
Values may be sent and summed in bfloat16 or wider, within the bound.
No kernel may reach another device: no remote copies, remote signals or barrier semaphores. Data moves between devices by JAX's collectives and lax.ppermute only.
A program may use at most 256 MiB of HBM per device.

v0:
```python
import math

import jax
import jax.numpy as jnp
from jax import lax
from jax.sharding import PartitionSpec as P

D = 768
HEADS = 12
HD = 64
GROUPS = 109


MARGIN = 0.3
LOGIT_SCALE = 30.0
NORM_EPS = 1e-12
UNIT_EPS = 1e-06
highest = lax.Precision.HIGHEST


def norm_forward(values, gain, shift):
    centred = values - jnp.mean(values, axis=-1, keepdims=True)
    inv_std = lax.rsqrt(jnp.mean(centred * centred, axis=-1, keepdims=True) + NORM_EPS)
    normed_hat = centred * inv_std
    return (normed_hat * gain + shift, normed_hat, inv_std)


def norm_backward(grad_out, normed_hat, inv_std, gain):
    grad_hat = grad_out * gain
    mean_grad = jnp.mean(grad_hat, axis=-1, keepdims=True)
    mean_cross = jnp.mean(grad_hat * normed_hat, axis=-1, keepdims=True)
    grad_in = inv_std * (grad_hat - mean_grad - normed_hat * mean_cross)
    return (grad_in, jnp.sum(grad_out * normed_hat, axis=0), jnp.sum(grad_out, axis=0))


def gelu_slope(values):
    normal_cdf = 0.5 * (1.0 + lax.erf(values * (1.0 / math.sqrt(2.0))))
    return normal_cdf + values * jnp.exp(-0.5 * values * values) * (1.0 / math.sqrt(2.0 * math.pi))


def to_heads(matrix, key_span):
    return matrix.reshape(-1, key_span, HEADS, HD)


def attend_scores(query_heads, key_heads, key_mask, factor):
    raw_scores = (
        jnp.einsum("bqhd,bkhd->bhqk", query_heads, key_heads, preferred_element_type=jnp.float32)
        * factor
    )
    return jnp.where(key_mask, raw_scores, -jnp.inf)


def outer_sum(left, right):
    return jnp.einsum("ri,rj->ij", left, right, preferred_element_type=jnp.float32)


def back_project(grad_rows, weight):
    return jnp.einsum("re,de->rd", grad_rows, weight, preferred_element_type=jnp.float32)


def shards(
    layer_input,
    pair_group,
    query_weight,
    query_bias,
    key_weight,
    value_weight,
    value_bias,
    out_weight,
    out_bias,
    mixer_gain,
    mixer_shift,
    up_weight,
    up_bias,
    down_weight,
    down_bias,
    final_gain,
    final_shift,
    upstream,
):
    tokens = layer_input[0]
    token_count = tokens.shape[0]
    seq_count = pair_group.shape[0]
    seq_len = token_count // seq_count
    key_span = 2 * seq_len
    factor = 1.0 / math.sqrt(HD)
    place = jnp.arange(key_span) // seq_len
    key_mask = place[:, None] == place[None, :]
    queries = (
        jnp.dot(tokens, query_weight, preferred_element_type=jnp.float32) + query_bias
    ).astype(jnp.bfloat16)
    keys_all = jnp.dot(tokens, key_weight, preferred_element_type=jnp.float32).astype(jnp.bfloat16)
    values_all = (
        jnp.dot(tokens, value_weight, preferred_element_type=jnp.float32) + value_bias
    ).astype(jnp.bfloat16)
    query_heads = to_heads(queries, key_span)
    key_heads = to_heads(keys_all, key_span)
    value_heads = to_heads(values_all, key_span)
    scores = attend_scores(query_heads, key_heads, key_mask, factor)
    row_top = jnp.max(scores, axis=-1, keepdims=True)
    log_total = row_top + jnp.log(jnp.sum(jnp.exp(scores - row_top), axis=-1, keepdims=True))
    probs_low = jnp.exp(scores - log_total).astype(jnp.bfloat16)
    context = jnp.einsum(
        "bhqk,bkhd->bqhd", probs_low, value_heads, preferred_element_type=jnp.float32
    )
    context = context.astype(jnp.bfloat16).reshape(token_count, D)
    attended = jnp.dot(context, out_weight, preferred_element_type=jnp.float32) + out_bias
    normed, hat_one, inv_one = norm_forward(
        tokens.astype(jnp.float32) + attended, mixer_gain, mixer_shift
    )
    normed_low = normed.astype(jnp.bfloat16)
    hidden_pre = jnp.dot(normed_low, up_weight, preferred_element_type=jnp.float32) + up_bias
    activated = jax.nn.gelu(hidden_pre, approximate=False).astype(jnp.bfloat16)
    branch = jnp.dot(activated, down_weight, preferred_element_type=jnp.float32) + down_bias
    final_rows, hat_two, inv_two = norm_forward(normed + branch, final_gain, final_shift)
    layer_output = final_rows.astype(jnp.bfloat16)[None]
    lead_rows = final_rows.reshape(seq_count, seq_len, D)[:, 0, :]
    lead_inv = lax.rsqrt(jnp.sum(lead_rows * lead_rows, axis=-1, keepdims=True) + UNIT_EPS)
    unit_rows = (lead_rows * lead_inv).astype(jnp.bfloat16)
    pairs_all = seq_count * lax.axis_size("dp")
    all_groups = lax.all_gather(pair_group, "dp", axis=0, tiled=True)
    everyone = lax.all_gather(unit_rows, ("stream", "dp"), axis=0, tiled=True).reshape(
        2, pairs_all, D
    )
    half_index = lax.axis_index("stream")
    offset = lax.axis_index("dp") * seq_count
    others = lax.dynamic_index_in_dim(everyone, 1 - half_index, 0, keepdims=False)
    group_range = jnp.arange(GROUPS, dtype=jnp.int32)
    own_hits = (pair_group[:, None] == group_range[None, :]).astype(jnp.float32)
    counts = lax.psum(jnp.sum(own_hits, axis=0), "dp")
    row_weight = pairs_all / GROUPS / jnp.sum(own_hits * counts[None, :], axis=1)
    sim_scores = LOGIT_SCALE * jnp.einsum(
        "id,jd->ij", unit_rows, others, preferred_element_type=jnp.float32
    )
    columns = jnp.arange(pairs_all, dtype=jnp.int32)
    diagonal = columns[None, :] == (offset + jnp.arange(seq_count, dtype=jnp.int32))[:, None]
    same_group = pair_group[:, None] == all_groups[None, :]
    logits = sim_scores - LOGIT_SCALE * MARGIN * diagonal.astype(jnp.float32)
    masked = jnp.where(same_group, logits, -jnp.inf)
    loss_top = jnp.max(masked, axis=1, keepdims=True)
    exp_terms = jnp.exp(masked - loss_top)
    row_sums = jnp.sum(exp_terms, axis=1, keepdims=True)
    own_logit = jnp.sum(jnp.where(diagonal, logits, 0.0), axis=1)
    row_loss = loss_top[:, 0] + jnp.log(row_sums[:, 0]) - own_logit
    loss_rows = (row_weight * row_loss)[None]
    dlogits = row_weight[:, None] * (exp_terms / row_sums - diagonal.astype(jnp.float32))
    grad_own = LOGIT_SCALE * jnp.dot(dlogits, others.astype(jnp.float32), precision=highest)
    grad_cols = LOGIT_SCALE * jnp.dot(dlogits.T, unit_rows.astype(jnp.float32), precision=highest)
    grad_terms = jnp.zeros((2, pairs_all, D), jnp.float32)
    grad_terms = lax.dynamic_update_slice(grad_terms, grad_cols[None], (1 - half_index, 0, 0))
    grad_terms = lax.dynamic_update_slice(grad_terms, grad_own[None], (half_index, offset, 0))
    unit_grad = lax.psum_scatter(
        grad_terms.reshape(2 * pairs_all, D), ("stream", "dp"), scatter_dimension=0, tiled=True
    )
    cross = jnp.sum(lead_rows * unit_grad, axis=-1, keepdims=True)
    lead_grad = lead_inv * unit_grad - lead_inv * lead_inv * lead_inv * cross * lead_rows
    final_grad = upstream[0].astype(jnp.float32).reshape(seq_count, seq_len, D)
    final_grad = final_grad.at[:, 0, :].add(lead_grad).reshape(token_count, D)
    dresid_two, final_gain_grad, final_shift_grad = norm_backward(
        final_grad, hat_two, inv_two, final_gain
    )
    dbranch = dresid_two.astype(jnp.bfloat16)
    down_weight_grad = outer_sum(activated, dbranch)
    down_bias_grad = jnp.sum(dbranch, axis=0, dtype=jnp.float32)
    dpre = (back_project(dbranch, down_weight) * gelu_slope(hidden_pre)).astype(jnp.bfloat16)
    up_weight_grad = outer_sum(normed_low, dpre)
    up_bias_grad = jnp.sum(dpre, axis=0, dtype=jnp.float32)
    dnormed = dresid_two + back_project(dpre, up_weight)
    dresid_one, mixer_gain_grad, mixer_shift_grad = norm_backward(
        dnormed, hat_one, inv_one, mixer_gain
    )
    datt = dresid_one.astype(jnp.bfloat16)
    out_weight_grad = outer_sum(context, datt)
    out_bias_grad = jnp.sum(datt, axis=0, dtype=jnp.float32)
    dcontext = back_project(datt, out_weight).astype(jnp.bfloat16)
    dcontext_heads = to_heads(dcontext, key_span)
    again = attend_scores(query_heads, key_heads, key_mask, factor)
    probs_f = jnp.exp(again - log_total)
    dprobs = jnp.einsum(
        "bqhd,bkhd->bhqk", dcontext_heads, value_heads, preferred_element_type=jnp.float32
    )
    row_dot = jnp.sum(probs_f * dprobs, axis=-1, keepdims=True)
    dscores = (probs_f * (dprobs - row_dot)).astype(jnp.bfloat16)
    dqueries = (
        jnp.einsum("bhqk,bkhd->bqhd", dscores, key_heads, preferred_element_type=jnp.float32)
        * factor
    )
    dqueries = dqueries.astype(jnp.bfloat16).reshape(token_count, D)
    dkeys = (
        jnp.einsum("bhqk,bqhd->bkhd", dscores, query_heads, preferred_element_type=jnp.float32)
        * factor
    )
    dkeys = dkeys.astype(jnp.bfloat16).reshape(token_count, D)
    dvalues = (
        jnp.einsum(
            "bhqk,bqhd->bkhd",
            probs_f.astype(jnp.bfloat16),
            dcontext_heads,
            preferred_element_type=jnp.float32,
        )
        .astype(jnp.bfloat16)
        .reshape(token_count, D)
    )
    query_weight_grad = outer_sum(tokens, dqueries)
    query_bias_grad = jnp.sum(dqueries, axis=0, dtype=jnp.float32)
    key_weight_grad = outer_sum(tokens, dkeys)
    value_weight_grad = outer_sum(tokens, dvalues)
    value_bias_grad = jnp.sum(dvalues, axis=0, dtype=jnp.float32)
    input_grad = (
        dresid_one
        + back_project(dqueries, query_weight)
        + back_project(dkeys, key_weight)
        + back_project(dvalues, value_weight)
    )
    local_grads = [
        query_weight_grad,
        query_bias_grad,
        key_weight_grad,
        value_weight_grad,
        value_bias_grad,
        out_weight_grad,
        out_bias_grad,
        mixer_gain_grad,
        mixer_shift_grad,
        up_weight_grad,
        up_bias_grad,
        down_weight_grad,
        down_bias_grad,
        final_gain_grad,
        final_shift_grad,
    ]
    flat_grads = jnp.concatenate([piece.reshape(-1) for piece in local_grads])
    total_len = flat_grads.shape[0]
    share_devices = lax.axis_size(("stream", "dp"))
    share_count = -(-total_len // share_devices)
    share_width = -(-share_count // 128) * 128
    flat_grads = flat_grads.reshape(share_devices, share_count)
    flat_grads = jnp.pad(flat_grads, ((0, 0), (0, share_width - share_count))).reshape(-1, 128)
    shares = lax.psum_scatter(flat_grads, ("stream", "dp"), scatter_dimension=0, tiled=True)
    reduced = lax.all_gather(
        shares.astype(jnp.bfloat16), ("stream", "dp"), axis=0, tiled=True
    ).astype(shares.dtype)
    reduced = reduced.reshape(share_devices, share_width)[:, :share_count].reshape(-1)
    summed = []
    cursor = 0
    for piece in local_grads:
        piece_len = piece.size
        summed.append(reduced[cursor : cursor + piece_len].reshape(piece.shape))
        cursor = cursor + piece_len
    return (
        layer_output,
        input_grad[None],
        loss_rows,
        summed[0],
        summed[1],
        summed[2],
        summed[3],
        summed[4],
        summed[5],
        summed[6],
        summed[7],
        summed[8],
        summed[9],
        summed[10],
        summed[11],
        summed[12],
        summed[13],
        summed[14],
    )


def solution(mesh):
    return jax.shard_map(
        shards,
        mesh=mesh,
        in_specs=(
            P("stream", "dp", None),
            P("dp"),
            P(),
            P(),
            P(),
            P(),
            P(),
            P(),
            P(),
            P(),
            P(),
            P(),
            P(),
            P(),
            P(),
            P(),
            P(),
            P("stream", "dp", None),
        ),
        out_specs=(
            P("stream", "dp", None),
            P("stream", "dp", None),
            P("stream", "dp"),
            P(),
            P(),
            P(),
            P(),
            P(),
            P(),
            P(),
            P(),
            P(),
            P(),
            P(),
            P(),
            P(),
            P(),
            P(),
        ),
        check_vma=False,
    )
```

profile of v0, /device:TPU:0, one launch (start us, length us, event | category | flops | bytes accessed | tf_op | source)
XLA Modules:
  0.0 1631.3 jit_solution(9747999156966175325)
XLA Ops:
  8.5 43.5 %psum.7 = f32[109]{0:T(128)S(1)} all-reduce(f32[109]{0:T(128)S(1)} %convert_reduce_fusion.5), channel_id=1, replica_groups=mesh['stream'=2,'dp'=16] {'dp'}, use_global_device_ids=true, to_apply=%region_8.9 | all-reduce | flops 109 | bytes 872 | tf_op jit(solution)/shard_map/psum | solution.py:130
  56.1 9.0 all-reduce.1
  65.3 4.3 add_convert_fusion
  97.5 34.9 %fusion.3 = (bf16[1024,3072]{1,0:T(8,128)(2,1)S(1)}, f32[1024,3072]{1,0:T(8,128)}) fusion(f32[3072]{0:T(1024)S(1)} %copy-done.61, bf16[768,3072]{1,0:T(8,128)(2,1)S(1)} %bitcast.204, f32[1024,768]{1,0:T(8,128)S(1)} %get-tuple-element.63, f32[768]{0:T(1024)S(1)} %copy-done.37, f32[768]{0:T(1024)S(1)} %copy-done.32, f32[1024]{0:T(1024)S(1)} %add_rsqrt_fusion.1, ...), kind=kOutput, calls=%fused_computation.6 | convolution fusion | flops 5043388416 | bytes 26765312 | tf_op jit(solution)/shard_map/dot_general | solution.py:112
  132.5 5.5 fusion.100
  141.3 69.7 %all_gather.10 = bf16[512,768]{1,0:T(8,128)(2,1)S(1)} all-gather(bf16[16,768]{1,0:T(8,128)(2,1)S(1)} %fusion.71), channel_id=1, replica_groups=mesh['stream'=2,'dp'=16] {'stream','dp'}, dimensions={0}, use_global_device_ids=true | all-gather | bytes 811008 | tf_op jit(solution)/shard_map/all_gather | solution.py:122
  215.9 3.4 convert.3
  219.3 93.5 %reduce-scatter.4.cloned.1.call-done = f32[16,768]{1,0:T(8,128)} async-done(((f32[512,768]{1,0:T(8,128)}), f32[16,768]{1,0:T(8,128)}) %reduce-scatter.4.cloned.1.call-update) | async-done | bytes 49168 | tf_op jit(solution)/shard_map/reduce_scatter | solution.py:152
  317.8 4.5 fusion.19
  323.4 4.1 convert_reduce_fusion.1
  327.5 10.3 fusion.86
  337.8 12.4 convert_reduce_fusion
  350.3 6.5 multiply_reduce_fusion.1
  356.8 8.7 convolution_bitcast_fusion
  374.8 6.4 convert_reduce_fusion.3
  385.8 4.9 fusion.41
  392.9 10.8 reshape.345
  403.7 9.6 copy.134
  422.9 3.0 copy.120
  425.9 3.2 reshape.342
  429.2 3.9 copy.114
  438.4 3.0 copy.118
  441.4 3.2 reshape.340
  444.6 4.7 convolution_bitcast_fusion.2
  449.3 3.0 copy.119
  452.4 3.2 reshape.341
  455.6 3.3 constant_dynamic-update-slice_fusion.9
  460.2 21.3 %dynamic-update-slice.6 = f32[7087104]{0:T(1024)} dynamic-update-slice(f32[7087104]{0:T(1024)} %constant_dynamic-update-slice_fusion.8, f32[589824]{0:T(1024)} %reshape.341, s32[]{} %constant.180) | dynamic-update-slice | bytes 4718596
  481.5 21.2 %dynamic-update-slice.7 = f32[7087104]{0:T(1024)} dynamic-update-slice(f32[7087104]{0:T(1024)} %dynamic-update-slice.6, f32[589824]{0:T(1024)} %reshape.342, s32[]{} %constant.181) | dynamic-update-slice | bytes 4718596
  504.0 20.3 %dynamic-update-slice.9 = f32[7087104]{0:T(1024)} dynamic-update-slice(f32[7087104]{0:T(1024)} %constant_dynamic-update-slice_fusion.7, f32[589824]{0:T(1024)S(1)} %reshape.343, s32[]{} %constant.183) | dynamic-update-slice | bytes 4718596
  528.2 80.3 %dynamic-update-slice.13 = f32[7087104]{0:T(1024)} dynamic-update-slice(f32[7087104]{0:T(1024)} %constant_dynamic-update-slice_fusion.4, f32[2359296]{0:T(1024)} %bitcast.172, s32[]{} %constant.187) | dynamic-update-slice | bytes 18874372
  609.9 80.6 %dynamic-update-slice.15 = f32[7087104]{0:T(1024)} dynamic-update-slice(f32[7087104]{0:T(1024)} %constant_dynamic-update-slice_fusion.3, f32[2359296]{0:T(1024)} %reshape.345, s32[]{} %constant.189) | dynamic-update-slice | bytes 18874372
  694.3 38.1 %reshape.346 = f32[32,221472]{1,0:T(8,128)} reshape(f32[7087104]{0:T(1024)} %constant_dynamic-update-slice_fusion) | data formatting | bytes 56696832 | tf_op jit(solution)/shard_map/reshape | solution.py:237
  732.3 20.9 %pad.6 = f32[32,221568]{1,0:T(8,128)} pad(f32[32,221472]{1,0:T(8,128)} %reshape.346, f32[]{:T(128)} %constant.120.clone.1), padding=0_0x0_96 | pad | bytes 56709124 | tf_op jit(solution)/shard_map/jit(_pad)/pad | solution.py:238
  753.2 25.4 %reshape.347 = f32[55392,128]{1,0:T(8,128)} reshape(f32[32,221568]{1,0:T(8,128)} %pad.6) | data formatting | bytes 56721408 | tf_op jit(solution)/shard_map/reshape | solution.py:238
  778.7 605.1 %fusion = f32[1744,128]{1,0:T(8,128)S(1)} fusion(f32[55392,128]{1,0:T(8,128)} %reshape.347), kind=kCustom, calls=%all-reduce-scatter | all-reduce-scatter fusion | flops 7143425 | bytes 29253632
  1385.1 3.1 collective-permute-done
  1390.5 2.9 fusion.27
  1396.1 3.3 add_bitcast_fusion
  1399.4 96.8 %all-gather.3.cloned.1.call-done = bf16[32,1731,128]{2,1,0:T(8,128)(2,1)} async-done(((bf16[1,1731,128]{2,1,0:T(8,128)(2,1)}), bf16[32,1731,128]{2,1,0:T(8,128)(2,1)}) %all-gather.3.cloned.1.call-update) | async-done | bytes 14180368 | tf_op jit(solution)/shard_map/all_gather | solution.py:240
  1496.2 12.8 copy.209
  1509.0 9.7 slice_convert_fusion
  1518.7 36.5 %reshape.361 = f32[7087104]{0:T(1024)} reshape(f32[32,221472]{1,0:T(8,128)} %slice_convert_fusion) | data formatting | bytes 56696832
  1557.9 8.3 slice.115
  1566.2 31.3 %slice.87 = f32[9228,768]{1,0:T(8,128)} reshape(f32[7087104]{0:T(1024)} %reshape.361) | data formatting | bytes 56696832 | tf_op jit(solution)/shard_map/slice | solution.py:248
  1597.5 8.1 slice.117
  1605.6 7.7 fusion.97
  1613.2 11.0 reshape.350
  (243 shorter events, 98.1 us)
Async XLA Ops:
  7.2 85.8 %copy-start = (bf16[768,768]{1,0:T(8,128)(2,1)S(1)}, bf16[768,768]{1,0:T(8,128)(2,1)}, u32[]{:S(2)}) copy-start(bf16[768,768]{1,0:T(8,128)(2,1)} %param.27) | copy-start | bytes 3538948
  7.2 305.6 %reduce-scatter.4.cloned.1.call-start = ((), (), s32[]{:S(2)}) async-start(), calls=%async_computation.1 | async-start | bytes 1622016 | tf_op jit(solution)/shard_map/reduce_scatter | solution.py:152
  65.2 24.3 %copy-start.29 = (pred[128,128]{0,1:T(8,128)(4,1)}, pred[128,128]{0,1:T(8,128)(4,1)S(1)}, u32[]{:S(2)}) copy-start(pred[128,128]{0,1:T(8,128)(4,1)S(1)} %broadcast_compare_fusion) | copy-start | bytes 49156
  69.6 3.4 copy-start.63
  78.9 10.7 copy-start.9
  93.2 39.3 %slice-start.2 = ((s8[4718592]{0:T(1024)(128)(4,1)}), s8[4194304]{0:T(1024)(128)(4,1)S(1)}, s32[]{:S(2)}) async-start(s8[4718592]{0:T(1024)(128)(4,1)} %bitcast.199), calls=%async_computation.5 | async-start | bytes 8388608
  94.9 37.6 %copy-start.5 = (f32[1024,768]{1,0:T(8,128)}, f32[1024,768]{1,0:T(8,128)S(1)}, u32[]{:S(2)}) copy-start(f32[1024,768]{1,0:T(8,128)S(1)} %get-tuple-element.63) | copy-start | bytes 9437188
  97.5 34.9 %slice-start.3 = ((s8[4718592]{0:T(1024)(128)(4,1)}), s8[524288]{0:T(1024)(128)(4,1)S(1)}, s32[]{:S(2)}) async-start(s8[4718592]{0:T(1024)(128)(4,1)} %bitcast.199), calls=%async_computation.6 | async-start | bytes 1048576
  97.5 34.9 %copy-start.65 = (f32[768]{0:T(1024)S(1)}, f32[768]{0:T(1024)}, u32[]{:S(2)}) copy-start(f32[768]{0:T(1024)} %param.34) | copy-start | bytes 9220
  132.4 5.5 copy-start.66
  138.8 72.3 %copy-start.39 = (s32[256]{0:T(256)S(1)}, s32[256]{0:T(256)}, u32[]{:S(2)}) copy-start(s32[256]{0:T(256)} %all-reduce.1) | copy-start | bytes 3076
  138.8 72.3 %copy-start.44 = (s32[16]{0:T(128)S(1)}, s32[16]{0:T(128)}, u32[]{:S(2)}) copy-start(s32[16]{0:T(128)} %param.21) | copy-start | bytes 196
  138.8 72.3 %copy-start.45 = (s32[16]{0:T(128)S(1)}, s32[16]{0:T(128)}, u32[]{:S(2)}) copy-start(s32[16]{0:T(128)} %iota_add_fusion) | copy-start | bytes 196
  138.8 72.8 %copy-start.53 = (f32[16]{0:T(128)S(1)}, f32[16]{0:T(128)}, u32[]{:S(2)}) copy-start(f32[16]{0:T(128)} %select_reduce_fusion.1) | copy-start | bytes 196
  140.6 71.6 %copy-start.18 = (f32[16,1,768]{2,1,0:T(1,128)}, f32[16,1,768]{2,1,0:T(1,128)S(1)}, u32[]{:S(2)}) copy-start(f32[16,1,768]{2,1,0:T(1,128)S(1)} %slice.104) | copy-start | bytes 147460
  141.2 70.9 %copy-start.46 = (f32[16]{0:T(128)}, f32[16]{0:T(128)S(1)}, u32[]{:S(2)}) copy-start(f32[16]{0:T(128)S(1)} %add_rsqrt_fusion.2) | copy-start | bytes 196
  141.3 70.8 %copy-start.31 = (bf16[16,768]{1,0:T(8,128)(2,1)}, bf16[16,768]{1,0:T(8,128)(2,1)S(1)}, u32[]{:S(2)}) copy-start(bf16[16,768]{1,0:T(8,128)(2,1)S(1)} %fusion.71) | copy-start | bytes 73732
  214.7 98.1 %copy-start.19 = (f32[16,1,768]{2,1,0:T(1,128)S(1)}, f32[16,1,768]{2,1,0:T(1,128)}, u32[]{:S(2)}) copy-start(f32[16,1,768]{2,1,0:T(1,128)} %copy-done.18) | copy-start | bytes 147460
  214.7 99.1 %copy-start.52 = (f32[16]{0:T(128)S(1)}, f32[16]{0:T(128)}, u32[]{:S(2)}) copy-start(f32[16]{0:T(128)} %copy-done.51) | copy-start | bytes 196
  214.7 99.1 %copy-start.47 = (f32[16]{0:T(128)S(1)}, f32[16]{0:T(128)}, u32[]{:S(2)}) copy-start(f32[16]{0:T(128)} %copy-done.46) | copy-start | bytes 196
  214.7 103.1 %copy-start.34 = (f32[768]{0:T(1024)S(1)}, f32[768]{0:T(1024)}, u32[]{:S(2)}) copy-start(f32[768]{0:T(1024)} %param.35) | copy-start | bytes 9220
  214.7 103.1 %copy-start.36 = (f32[1024]{0:T(1024)S(1)}, f32[1024]{0:T(1024)}, u32[]{:S(2)}) copy-start(f32[1024]{0:T(1024)} %copy-done.35) | copy-start | bytes 12292
  215.8 1280.4 %all-gather.3.cloned.1.call-start = ((), (), s32[]{:S(2)}) async-start(), calls=%async_computation.2 | async-start | bytes 14665728 | tf_op jit(solution)/shard_map/all_gather | solution.py:240
  317.8 4.5 copy-start.3
  323.4 14.4 slice-start.4
  327.5 10.3 slice-start.5
  327.5 10.3 copy-start.62
  327.5 22.8 %slice-start.8 = ((s8[4718592]{0:T(1024)(128)(4,1)}), s8[4194304]{0:T(1024)(128)(4,1)S(1)}, s32[]{:S(2)}) async-start(s8[4718592]{0:T(1024)(128)(4,1)} %bitcast.205), calls=%async_computation.11 | async-start | bytes 8388608
  337.8 12.5 copy-start.6
  337.8 12.5 slice-start.9
  350.3 6.5 copy-start.38
  366.6 3.1 copy-start.7
  374.3 6.9 slice-start
  374.8 6.5 slice-start.1
  374.8 6.5 copy-start.10
  385.8 4.9 copy-start.16
  416.2 3.9 copy-start.57
  429.2 3.9 copy-start.17
  429.2 6.3 copy-start.58
  502.7 22.9 %copy-start.50 = (f32[768]{0:T(1024)S(1)}, f32[768]{0:T(1024)}, u32[]{:S(2)}) copy-start(f32[768]{0:T(1024)} %get-tuple-element.32) | copy-start | bytes 9220
  502.7 24.2 %copy-start.49 = (f32[768]{0:T(1024)S(1)}, f32[768]{0:T(1024)}, u32[]{:S(2)}) copy-start(f32[768]{0:T(1024)} %get-tuple-element.37) | copy-start | bytes 9220
  528.2 80.3 %copy-start.43 = (f32[3072]{0:T(1024)S(1)}, f32[3072]{0:T(1024)}, u32[]{:S(2)}) copy-start(f32[3072]{0:T(1024)} %get-tuple-element.77) | copy-start | bytes 36868
  609.9 80.6 %copy-start.41 = (f32[768]{0:T(1024)S(1)}, f32[768]{0:T(1024)}, u32[]{:S(2)}) copy-start(f32[768]{0:T(1024)} %get-tuple-element.40) | copy-start | bytes 9220
  609.9 81.9 %copy-start.42 = (f32[768]{0:T(1024)S(1)}, f32[768]{0:T(1024)}, u32[]{:S(2)}) copy-start(f32[768]{0:T(1024)} %get-tuple-element.30) | copy-start | bytes 9220
  609.9 83.2 %copy-start.40 = (f32[768]{0:T(1024)S(1)}, f32[768]{0:T(1024)}, u32[]{:S(2)}) copy-start(f32[768]{0:T(1024)} %get-tuple-element.35) | copy-start | bytes 9220
  778.7 611.8 %copy-start.24 = (bf16[8,128,12,64]{1,0,3,2:T(8,128)(2,1)S(1)}, bf16[8,128,12,64]{1,0,3,2:T(8,128)(2,1)}, u32[]{:S(2)}) copy-start(bf16[8,128,12,64]{1,0,3,2:T(8,128)(2,1)} %copy-done.23) | copy-start | bytes 4718596
  1383.8 4.4 collective-permute-start
  1613.2 11.0 copy-start.1
  (32 other events, 63.5 us)
Sparse Core Ops, SparseCore 0:
  216.0 96.8 reduce-scatter.3
  1390.6 105.5 all-gather.2
where the time goes:
time: 1650 us; the launch traced here: 1630 us
  blocking collectives  727 us (44%)
  local copies, waits for them, and re-layouts  523 us (32%)
  waiting for transfers between devices  193 us (12%)
  matrix products  133 us (8%)
  other arithmetic  37.2 us (2%)
    unnamed x2, blocking collectives  614 us
    unnamed x181, local copies, waits for them, and re-layouts  316 us
    all_gather x1, waiting for transfers between devices, shards(): lax.all_gather(shares.astype(jnp.bfloat16), ('stream', 'dp'), axis=0, til...  96.8 us
    reduce_scatter x1, waiting for transfers between devices, shards(): lax.psum_scatter(grad_terms.reshape(2 * pairs_all, D), ('stream', 'dp'),...  93.5 us
    all_gather x1, blocking collectives, shards(): lax.all_gather(unit_rows, ('stream', 'dp'), axis=0, tiled=True)  69.7 us
    slice x6, local copies, waits for them, and re-layouts, shards(): summed.append(reduced[cursor:cursor + piece_len].reshape(piece.shape))  58 us
    psum x1, blocking collectives, shards(): counts = lax.psum(jnp.sum(own_hits, axis=0), 'dp')  43.5 us
    reshape x1, local copies, waits for them, and re-layouts, shards(): flat_grads = flat_grads.reshape(share_devices, share_count)  38.1 us
  transfers between devices with their start and end apart: 3, of which 3 were waited for; matrix products, arithmetic and copies ran while one was open for 1% of the time, Pallas kernels for 0%

commit v1 on v0

--- a/solution.py
+++ b/solution.py
@@ -56,6 +56,99 @@
 
 def back_project(grad_rows, weight):
     return jnp.einsum("re,de->rd", grad_rows, weight, preferred_element_type=jnp.float32)
+
+
+def chip_partner(bit_zero, bit_one):
+    chips = lax.axis_size("dp")
+    return [
+        (half * chips + chip, half * chips + (chip ^ (bit_zero if half == 0 else bit_one)))
+        for half in range(2)
+        for chip in range(chips)
+    ]
+
+
+def core_partner():
+    chips = lax.axis_size("dp")
+    return [(half * chips + chip, (1 - half) * chips + chip) for half in range(2) for chip in range(chips)]
+
+
+def swap(piece, pairs):
+    return lax.ppermute(piece, ("stream", "dp"), pairs)
+
+
+def add_low(left, right):
+    return (left.astype(jnp.float32) + right.astype(jnp.float32)).astype(jnp.bfloat16)
+
+
+def all_sum(blocks):
+    half = lax.axis_index("stream")
+    chip = lax.axis_index("dp")
+    low, high = chip & 1, (chip >> 1) & 1
+    first = jnp.where(half == 0, low, high)
+    second = jnp.where(half == 0, high, low)
+    steps = [(half, core_partner()), (first, chip_partner(1, 2)), (second, chip_partner(2, 1))]
+    for mine, pairs in steps:
+        take = lambda index: lax.dynamic_index_in_dim(blocks, index, 0, keepdims=False)
+        blocks = add_low(take(mine), swap(take(1 - mine), pairs))
+    bits = [1 << k for k in range(2, lax.axis_size("dp").bit_length() - 1)]
+    for bit_zero, bit_one in zip(bits, bits[::-1], strict=True):
+        blocks = add_low(blocks, swap(blocks, chip_partner(bit_zero, bit_one)))
+    for mine, pairs in steps[::-1]:
+        other = swap(blocks, pairs)
+        blocks = jnp.where(mine == 0, jnp.stack([blocks, other]), jnp.stack([other, blocks]))
+    return blocks
+
+
+def gather_rows(rows):
+    chips = lax.axis_size("dp")
+    bit = 1
+    while bit < chips:
+        rows = jnp.concatenate([rows, swap(rows, chip_partner(bit, bit))])
+        bit *= 2
+    return rows, swap(rows, core_partner())
+
+
+def feed_forward(normed_low, up_weight, up_bias, down_weight, down_bias):
+    hidden_pre = jnp.dot(normed_low, up_weight, preferred_element_type=jnp.float32) + up_bias
+    activated = jax.nn.gelu(hidden_pre, approximate=False).astype(jnp.bfloat16)
+    branch = jnp.dot(activated, down_weight, preferred_element_type=jnp.float32) + down_bias
+    return hidden_pre, activated, branch
+
+
+def pair_loss(lead_rows, pair_group):
+    seq_count = pair_group.shape[0]
+    pairs_all = seq_count * lax.axis_size("dp")
+    lead_inv = lax.rsqrt(jnp.sum(lead_rows * lead_rows, axis=-1, keepdims=True) + UNIT_EPS)
+    unit_rows = (lead_rows * lead_inv).astype(jnp.bfloat16)
+    ids = jnp.broadcast_to(pair_group.astype(jnp.bfloat16)[:, None], (seq_count, 128))
+    own_side, other_side = gather_rows(jnp.concatenate([unit_rows, ids], axis=1))
+    groups = own_side[:, D].astype(jnp.float32)
+    same_group = groups[:, None] == groups[None, :]
+    row_weight = pairs_all / GROUPS / jnp.sum(same_group.astype(jnp.float32), axis=1)
+    sim_scores = LOGIT_SCALE * jnp.einsum(
+        "id,jd->ij", own_side[:, :D], other_side[:, :D], preferred_element_type=jnp.float32
+    )
+    place = jnp.arange(pairs_all, dtype=jnp.int32)
+    diagonal = (place[:, None] == place[None, :]).astype(jnp.float32)
+    logits = sim_scores - LOGIT_SCALE * MARGIN * diagonal
+    masked = jnp.where(same_group, logits, -jnp.inf)
+    col_top = jnp.max(masked, axis=0, keepdims=True)
+    col_lse = col_top + jnp.log(jnp.sum(jnp.exp(masked - col_top), axis=0, keepdims=True))
+    own = masked[:seq_count]
+    row_top = jnp.max(own, axis=1, keepdims=True)
+    row_lse = row_top + jnp.log(jnp.sum(jnp.exp(own - row_top), axis=1, keepdims=True))
+    own_diag = diagonal[:seq_count]
+    own_logit = jnp.sum(logits[:seq_count] * own_diag, axis=1)
+    loss_rows = (row_weight[:seq_count] * (row_lse[:, 0] - own_logit))[None]
+    dsims = row_weight[:seq_count, None] * (jnp.exp(own - row_lse) - own_diag) + row_weight[
+        None, :
+    ] * (jnp.exp(own - col_lse) - own_diag)
+    unit_grad = LOGIT_SCALE * jnp.dot(
+        dsims, other_side[:, :D].astype(jnp.float32), precision=highest
+    )
+    cross = jnp.sum(lead_rows * unit_grad, axis=-1, keepdims=True)
+    lead_grad = lead_inv * unit_grad - lead_inv * lead_inv * lead_inv * cross * lead_rows
+    return loss_rows, lead_grad
 
 
 def shards(
@@ -109,51 +202,17 @@
         tokens.astype(jnp.float32) + attended, mixer_gain, mixer_shift
     )
     normed_low = normed.astype(jnp.bfloat16)
-    hidden_pre = jnp.dot(normed_low, up_weight, preferred_element_type=jnp.float32) + up_bias
-    activated = jax.nn.gelu(hidden_pre, approximate=False).astype(jnp.bfloat16)
-    branch = jnp.dot(activated, down_weight, preferred_element_type=jnp.float32) + down_bias
+    lead_normed = normed.reshape(seq_count, seq_len, D)[:, 0, :]
+    _, _, lead_branch = feed_forward(
+        lead_normed.astype(jnp.bfloat16), up_weight, up_bias, down_weight, down_bias
+    )
+    lead_rows, _, _ = norm_forward(lead_normed + lead_branch, final_gain, final_shift)
+    loss_rows, lead_grad = pair_loss(lead_rows, pair_group)
+    hidden_pre, activated, branch = feed_forward(
+        normed_low, up_weight, up_bias, down_weight, down_bias
+    )
     final_rows, hat_two, inv_two = norm_forward(normed + branch, final_gain, final_shift)
     layer_output = final_rows.astype(jnp.bfloat16)[None]
-    lead_rows = final_rows.reshape(seq_count, seq_len, D)[:, 0, :]
-    lead_inv = lax.rsqrt(jnp.sum(lead_rows * lead_rows, axis=-1, keepdims=True) + UNIT_EPS)
-    unit_rows = (lead_rows * lead_inv).astype(jnp.bfloat16)
-    pairs_all = seq_count * lax.axis_size("dp")
-    all_groups = lax.all_gather(pair_group, "dp", axis=0, tiled=True)
-    everyone = lax.all_gather(unit_rows, ("stream", "dp"), axis=0, tiled=True).reshape(
-        2, pairs_all, D
-    )
-    half_index = lax.axis_index("stream")
-    offset = lax.axis_index("dp") * seq_count
-    others = lax.dynamic_index_in_dim(everyone, 1 - half_index, 0, keepdims=False)
-    group_range = jnp.arange(GROUPS, dtype=jnp.int32)
-    own_hits = (pair_group[:, None] == group_range[None, :]).astype(jnp.float32)
-    counts = lax.psum(jnp.sum(own_hits, axis=0), "dp")
-    row_weight = pairs_all / GROUPS / jnp.sum(own_hits * counts[None, :], axis=1)
-    sim_scores = LOGIT_SCALE * jnp.einsum(
-        "id,jd->ij", unit_rows, others, preferred_element_type=jnp.float32
-    )
-    columns = jnp.arange(pairs_all, dtype=jnp.int32)
-    diagonal = columns[None, :] == (offset + jnp.arange(seq_count, dtype=jnp.int32))[:, None]
-    same_group = pair_group[:, None] == all_groups[None, :]
-    logits = sim_scores - LOGIT_SCALE * MARGIN * diagonal.astype(jnp.float32)
-    masked = jnp.where(same_group, logits, -jnp.inf)
-    loss_top = jnp.max(masked, axis=1, keepdims=True)
-    exp_terms = jnp.exp(masked - loss_top)
-    row_sums = jnp.sum(exp_terms, axis=1, keepdims=True)
-    own_logit = jnp.sum(jnp.where(diagonal, logits, 0.0), axis=1)
-    row_loss = loss_top[:, 0] + jnp.log(row_sums[:, 0]) - own_logit
-    loss_rows = (row_weight * row_loss)[None]
-    dlogits = row_weight[:, None] * (exp_terms / row_sums - diagonal.astype(jnp.float32))
-    grad_own = LOGIT_SCALE * jnp.dot(dlogits, others.astype(jnp.float32), precision=highest)
-    grad_cols = LOGIT_SCALE * jnp.dot(dlogits.T, unit_rows.astype(jnp.float32), precision=highest)
-    grad_terms = jnp.zeros((2, pairs_all, D), jnp.float32)
-    grad_terms = lax.dynamic_update_slice(grad_terms, grad_cols[None], (1 - half_index, 0, 0))
-    grad_terms = lax.dynamic_update_slice(grad_terms, grad_own[None], (half_index, offset, 0))
-    unit_grad = lax.psum_scatter(
-        grad_terms.reshape(2 * pairs_all, D), ("stream", "dp"), scatter_dimension=0, tiled=True
-    )
-    cross = jnp.sum(lead_rows * unit_grad, axis=-1, keepdims=True)
-    lead_grad = lead_inv * unit_grad - lead_inv * lead_inv * lead_inv * cross * lead_rows
     final_grad = upstream[0].astype(jnp.float32).reshape(seq_count, seq_len, D)
     final_grad = final_grad.at[:, 0, :].add(lead_grad).reshape(token_count, D)
     dresid_two, final_gain_grad, final_shift_grad = norm_backward(
@@ -212,60 +271,54 @@
         + back_project(dkeys, key_weight)
         + back_project(dvalues, value_weight)
     )
-    local_grads = [
-        query_weight_grad,
-        query_bias_grad,
-        key_weight_grad,
-        value_weight_grad,
-        value_bias_grad,
-        out_weight_grad,
-        out_bias_grad,
-        mixer_gain_grad,
-        mixer_shift_grad,
-        up_weight_grad,
-        up_bias_grad,
-        down_weight_grad,
-        down_bias_grad,
-        final_gain_grad,
-        final_shift_grad,
-    ]
-    flat_grads = jnp.concatenate([piece.reshape(-1) for piece in local_grads])
-    total_len = flat_grads.shape[0]
-    share_devices = lax.axis_size(("stream", "dp"))
-    share_count = -(-total_len // share_devices)
-    share_width = -(-share_count // 128) * 128
-    flat_grads = flat_grads.reshape(share_devices, share_count)
-    flat_grads = jnp.pad(flat_grads, ((0, 0), (0, share_width - share_count))).reshape(-1, 128)
-    shares = lax.psum_scatter(flat_grads, ("stream", "dp"), scatter_dimension=0, tiled=True)
-    reduced = lax.all_gather(
-        shares.astype(jnp.bfloat16), ("stream", "dp"), axis=0, tiled=True
-    ).astype(shares.dtype)
-    reduced = reduced.reshape(share_devices, share_width)[:, :share_count].reshape(-1)
-    summed = []
-    cursor = 0
-    for piece in local_grads:
-        piece_len = piece.size
-        summed.append(reduced[cursor : cursor + piece_len].reshape(piece.shape))
-        cursor = cursor + piece_len
+    low = lambda piece: piece.astype(jnp.bfloat16)
+    wide = down_bias.shape[0] * 4
+    small = jnp.concatenate(
+        [
+            up_bias_grad,
+            query_bias_grad,
+            value_bias_grad,
+            out_bias_grad,
+            mixer_gain_grad,
+            mixer_shift_grad,
+            down_bias_grad,
+            final_gain_grad,
+            final_shift_grad,
+        ]
+    )
+    small = jnp.pad(small, (0, 8 * wide - small.shape[0])).reshape(2, 2, 2, 1, wide)
+    down_sum = all_sum(low(down_weight_grad).reshape(2, 2, 2, -1, D))
+    up_sum = all_sum(low(up_weight_grad).reshape(2, 2, 2, -1, up_weight.shape[1]))
+    square = jnp.concatenate(
+        [low(query_weight_grad), low(key_weight_grad), low(value_weight_grad), low(out_weight_grad)], axis=1
+    ).reshape(2, 2, 2, -1, wide)
+    square_sum = all_sum(jnp.concatenate([square, low(small)], axis=3))
+    full = jnp.float32
+    down_out = down_sum.reshape(down_weight.shape).astype(full)
+    up_out = up_sum.reshape(up_weight.shape).astype(full)
+    squares = square_sum[:, :, :, :-1].reshape(D, wide).astype(full)
+    smalls = square_sum[:, :, :, -1].reshape(-1).astype(full)
+    hidden = up_bias.shape[0]
+    vector = lambda k: smalls[hidden + k * D : hidden + (k + 1) * D]
     return (
         layer_output,
         input_grad[None],
         loss_rows,
-        summed[0],
-        summed[1],
-        summed[2],
-        summed[3],
-        summed[4],
-        summed[5],
-        summed[6],
-        summed[7],
-        summed[8],
-        summed[9],
-        summed[10],
-        summed[11],
-        summed[12],
-        summed[13],
-        summed[14],
+        squares[:, :D],
+        vector(0),
+        squares[:, D : 2 * D],
+        squares[:, 2 * D : 3 * D],
+        vector(1),
+        squares[:, 3 * D :],
+        vector(2),
+        vector(3),
+        vector(4),
+        up_out,
+        smalls[:hidden],
+        down_out,
+        vector(5),
+        vector(6),
+        vector(7),
     )
 
 

time: 1650 us -> 445 us (0.27)
  blocking collectives: 727 us -> 0 us
  local copies, waits for them, and re-layouts: 523 us -> 62.1 us
  starting transfers between devices: 1.38 us -> 45 us
  waiting for transfers between devices: 193 us -> 151 us
    unnamed x2 -> x0, blocking collectives: 614 us -> none
    unnamed x181 -> x157, local copies, waits for them, and re-layouts: 316 us -> 18.6 us
    ppermute x0 -> x29, waiting for transfers between devices: none -> 151 us  [swap(): return lax.ppermute(piece, ('stream', 'dp'), pairs)]
    reshape x8 -> x0, local copies, waits for them, and re-layouts: 97.8 us -> none  [the longest x1 38.1 us: shards(): flat_grads = flat_grads.reshape(share_devices, share_count)]
    all_gather x1 -> x0, waiting for transfers between devices: 96.8 us -> none  [shards(): lax.all_gather(shares.astype(jnp.bfloat16), ('stream', 'dp'), axis=0, til...]
    reduce_scatter x1 -> x0, waiting for transfers between devices: 93.5 us -> none  [shards(): lax.psum_scatter(grad_terms.reshape(2 * pairs_all, D), ('stream', 'dp'),...]
    all_gather x1 -> x0, blocking collectives: 69.7 us -> none  [shards(): lax.all_gather(unit_rows, ('stream', 'dp'), axis=0, tiled=True)]
    slice x7 -> x5, local copies, waits for them, and re-layouts: 58 us -> 5.63 us  [the longest x1 3.88 us: shards(): squares[:, 3 * D:]]
  transfers between devices with their start and end apart: 3 -> 29, of which waited for: 3 -> 14; matrix products, arithmetic and copies ran while one was open for 1% -> 23% of each run, Pallas kernels for 0% -> 0%
where the time goes in v1:
time: 445 us; the launch traced here: 440 us
  waiting for transfers between devices  151 us (34%)
  matrix products  127 us (29%)
  local copies, waits for them, and re-layouts  62.1 us (14%)
  other arithmetic  53 us (12%)
  starting transfers between devices  45 us (10%)
    ppermute x29, waiting for transfers between devices, swap(): return lax.ppermute(piece, ('stream', 'dp'), pairs)  151 us
    ppermute x29, starting transfers between devices, swap(): return lax.ppermute(piece, ('stream', 'dp'), pairs)  45 us
    dot_general x1, matrix products, feed_forward(): jnp.dot(normed_low, up_weight, preferred_element_type=jnp.float32) + up_bias  35.1 us
    dot_general x6, matrix products, back_project(): jnp.einsum('re,de->rd', grad_rows, weight, preferred_element_type=jnp.flo...  33.2 us
    dot_general x6, matrix products, outer_sum(): jnp.einsum('ri,rj->ij', left, right, preferred_element_type=jnp.float32)  21.3 us
    unnamed x157, local copies, waits for them, and re-layouts  18.6 us
    dot_general x2, matrix products, feed_forward(): jnp.dot(activated, down_weight, preferred_element_type=jnp.float32)  10.8 us
  transfers between devices with their start and end apart: 29, of which 14 were waited for; matrix products, arithmetic and copies ran while one was open for 23% of the time, Pallas kernels for 0%

profile of v1, /device:TPU:0, one launch (start us, length us, event | category | flops | bytes accessed | tf_op | source)
XLA Modules:
  0.0 440.1 jit_solution(8124886641501285091)
XLA Ops:
  0.7 3.2 add_convert_fusion.2
  7.8 2.5 convolution_convert_fusion.5
  10.3 2.6 copy.110
  12.9 3.2 copy.150
  16.1 2.5 add_convert_fusion.1
  18.6 3.1 copy.109
  35.9 5.5 %fusion.223 = (f32[16]{0:T(128)S(1)}, f32[16,768]{1,0:T(8,128)S(1)}) fusion(f32[768]{0:T(1024)S(1)} %copy-done.45, bf16[3072,768]{1,0:T(8,128)(2,1)} %param.33, bf16[768,3072]{1,0:T(8,128)(2,1)} %param.31, f32[3072]{0:T(1024)S(1)} %copy-done.43, f32[16,1,768]{2,1,0:T(1,128)S(1)} %slice.128), kind=kOutput, calls=%fused_computation.351 | convolution fusion | flops 154288112 | bytes 9550912 | tf_op jit(solution)/shard_map/dot_general | solution.py:114
  42.1 3.0 collective-permute-start
  45.1 35.1 %fusion.2 = (bf16[1024,3072]{1,0:T(8,128)(2,1)S(1)}, f32[1024,3072]{1,0:T(8,128)}) fusion(f32[3072]{0:T(1024)S(1)} %copy-done.43, bf16[768,3072]{1,0:T(8,128)(2,1)} %param.31, f32[1024,768]{1,0:T(8,128)} %copy-done.18), kind=kOutput, calls=%fused_computation.4 | convolution fusion | flops 5040242688 | bytes 26750976 | tf_op jit(solution)/shard_map/dot_general | solution.py:112
  82.4 5.3 %fusion.226 = (f32[1024]{0:T(1024)S(1)}, f32[1024,768]{1,0:T(8,128)S(1)}) fusion(f32[1024,768]{1,0:T(8,128)S(1)} %copy-done.19, f32[768]{0:T(1024)S(1)} %copy-done.45, bf16[1024,3072]{1,0:T(8,128)(2,1)S(1)} %get-tuple-element.76, bf16[3072,768]{1,0:T(8,128)(2,1)S(1)} %bitcast.309), kind=kOutput, calls=%fused_computation.352 | convolution fusion | flops 4834196480 | bytes 17308672 | tf_op jit(solution)/shard_map/dot_general | solution.py:114
  89.4 3.2 collective-permute-done.2
  92.6 2.7 collective-permute-start.3
  95.3 8.9 %collective-permute-done.3 = bf16[128,896]{1,0:T(8,128)(2,1)S(1)} collective-permute-done((bf16[128,896]{1,0:T(8,128)(2,1)S(1)}, bf16[128,896]{1,0:T(8,128)(2,1)S(1)}, u32[]{:S(2)}, u32[]{:S(2)}) %collective-permute-start.3) | collective-permute-done | bytes 229408 | tf_op jit(solution)/shard_map/ppermute | solution.py:76
  113.8 4.0 fusion.21
  117.9 3.5 convert_reduce_fusion.2
  122.0 14.4 %fusion.227 = (bf16[3072]{0:T(1024)(128)(2,1)S(1)}, bf16[1024,3072]{1,0:T(8,128)(2,1)}) fusion(f32[1024,3072]{1,0:T(8,128)} %get-tuple-element.77, f32[3072]{0:T(1024)S(1)} %copy-done.43, bf16[3072,768]{1,0:T(8,128)(2,1)S(1)} %bitcast.311, f32[1024,768]{1,0:T(8,128)S(1)} %get-tuple-element.39), kind=kOutput, calls=%fused_computation.353 | convolution fusion | flops 4870370304 | bytes 26757120 | tf_op jit(solution)/shard_map/re,de->rd/dot_general | solution.py:58
  136.5 8.3 %multiply_reduce_fusion.1 = (bf16[768]{0:T(1024)(128)(2,1)S(1)}, f32[1024]{0:T(1024)S(1)}, f32[1024]{0:T(1024)S(1)}, bf16[768]{0:T(1024)(128)(2,1)S(1)}, f32[1024,768]{1,0:T(8,128)S(1)}) fusion(f32[1024,768]{1,0:T(8,128)S(1)} %copy-done.5, f32[1024]{0:T(1024)S(1)} %copy-done.40, f32[1024]{0:T(1024)S(1)} %copy-done.37, f32[768]{0:T(1024)S(1)} %copy-done.42, ...), kind=kOutput, calls=%fused_computation.56 | convolution fusion | flops 4839698432 | bytes 20469760 | tf_op jit(solution)/shard_map/re,de->rd/dot_general | solution.py:58
  147.6 2.6 convolution_convert_fusion.3
  150.2 2.7 copy.119
  154.8 5.3 %multiply_reduce_fusion = (f32[8,12,128]{2,1,0:T(8,128)S(1)}, f32[8,12,128,128]{2,3,1,0:T(8,128)S(1)}) fusion(f32[8,12,128,128]{2,3,1,0:T(8,128)} %copy-done.1, f32[8,12,128]{2,1,0:T(8,128)S(1)} %copy-done.32, pred[128,128]{0,1:T(8,128)(4,1)S(1)} %copy-done.34, bf16[8,128,12,64]{1,0,3,2:T(8,128)(2,1)S(1)} %bitcast.274, ...), kind=kOutput, calls=%fused_computation.29 | convolution fusion | flops 209178624 | bytes 15843328 | tf_op jit(solution)/shard_map/bqhd,bkhd->bhqk/dot_general | solution.py:238
  162.5 3.8 fusion.70
  172.0 8.4 %convolution_convert_fusion.1 = bf16[768,3072]{1,0:T(8,128)(2,1)S(1)} fusion(bf16[1024,3072]{1,0:T(8,128)(2,1)} %get-tuple-element.84, f32[1024,768]{1,0:T(8,128)S(1)} %copy-done.20), kind=kOutput, calls=%fused_computation.37 | convolution fusion | flops 4834983936 | bytes 14155776 | tf_op jit(solution)/shard_map/ri,rj->ij/dot_general | solution.py:54
  180.5 7.2 %convolution_convert_fusion = bf16[3072,768]{1,0:T(8,128)(2,1)} fusion(bf16[1024,3072]{1,0:T(8,128)(2,1)S(1)} %bitcast.329, f32[1024,768]{1,0:T(8,128)S(1)} %copy-done.22), kind=kOutput, calls=%fused_computation.36 | convolution fusion | flops 4834983936 | bytes 14155776 | tf_op jit(solution)/shard_map/ri,rj->ij/dot_general | solution.py:54
  200.2 6.6 %copy.131 = bf16[768,3072]{1,0:T(8,128)(2,1)} copy(bf16[768,3072]{0,1:T(8,128)(2,1)} %pad_maximum_fusion) | data formatting | bytes 9437184 | tf_op jit(solution)/shard_map/concatenate | solution.py:292
  208.8 3.4 dynamic-slice_bitcast_fusion
  218.5 3.0 fusion.38
  221.5 3.3 add_bitcast_fusion
  224.9 2.6 fusion.19
  234.6 9.2 %collective-permute-done.14 = bf16[2,96,3072]{2,1,0:T(8,128)(2,1)S(1)} collective-permute-done((bf16[2,96,3072]{2,1,0:T(8,128)(2,1)S(1)}, bf16[2,96,3072]{2,1,0:T(8,128)(2,1)S(1)}, u32[]{:S(2)}, u32[]{:S(2)}) %collective-permute-start.14) | collective-permute-done | bytes 1179680 | tf_op jit(solution)/shard_map/ppermute | solution.py:76
  245.2 17.6 %collective-permute-done.22 = bf16[2,384,768]{2,1,0:T(8,128)(2,1)S(1)} collective-permute-done((bf16[2,384,768]{2,1,0:T(8,128)(2,1)S(1)}, bf16[2,384,768]{2,1,0:T(8,128)(2,1)S(1)}, u32[]{:S(2)}, u32[]{:S(2)}) %collective-permute-start.22) | collective-permute-done | bytes 1179680 | tf_op jit(solution)/shard_map/ppermute | solution.py:76
  263.7 18.2 %collective-permute-done.6 = bf16[2,97,3072]{2,0,1:T(2,128)(2,1)S(1)} collective-permute-done((bf16[2,97,3072]{2,0,1:T(2,128)(2,1)S(1)}, bf16[2,97,3072]{2,0,1:T(2,128)(2,1)S(1)}, u32[]{:S(2)}, u32[]{:S(2)}) %collective-permute-start.6) | collective-permute-done | bytes 1191968 | tf_op jit(solution)/shard_map/ppermute | solution.py:76
  285.4 7.4 %collective-permute-done.7 = bf16[97,3072]{1,0:T(8,128)(2,1)S(1)} collective-permute-done((bf16[97,3072]{1,0:T(8,128)(2,1)S(1)}, bf16[97,3072]{1,0:T(8,128)(2,1)S(1)}, u32[]{:S(2)}, u32[]{:S(2)}) %collective-permute-start.7) | collective-permute-done | bytes 596000 | tf_op jit(solution)/shard_map/ppermute | solution.py:76
  293.8 3.9 collective-permute-done.16
  297.8 3.9 collective-permute-start.17
  301.7 17.0 %collective-permute-done.24 = bf16[384,768]{1,0:T(8,128)(2,1)S(1)} collective-permute-done((bf16[384,768]{1,0:T(8,128)(2,1)S(1)}, bf16[384,768]{1,0:T(8,128)(2,1)S(1)}, u32[]{:S(2)}, u32[]{:S(2)}) %collective-permute-start.24) | collective-permute-done | bytes 589856 | tf_op jit(solution)/shard_map/ppermute | solution.py:76
  318.9 11.0 %collective-permute-start.25 = (bf16[384,768]{1,0:T(8,128)(2,1)S(1)}, bf16[384,768]{1,0:T(8,128)(2,1)S(1)}, u32[]{:S(2)}, u32[]{:S(2)}) collective-permute-start(bf16[384,768]{1,0:T(8,128)(2,1)S(1)} %add_convert_fusion.6), channel_id=1, source_target_pairs={{0,8},{1,9},{2,10},{3,11},{4,12},{5,13},{6,14},{7,15},{8,0},{9,1},... | collective-permute-start | bytes 1769480 | tf_op jit(solution)/shard_map/ppermute | solution.py:76
  329.8 18.6 %collective-permute-done.8 = bf16[97,3072]{1,0:T(8,128)(2,1)S(1)} collective-permute-done((bf16[97,3072]{1,0:T(8,128)(2,1)S(1)}, bf16[97,3072]{1,0:T(8,128)(2,1)S(1)}, u32[]{:S(2)}, u32[]{:S(2)}) %collective-permute-start.8) | collective-permute-done | bytes 596000 | tf_op jit(solution)/shard_map/ppermute | solution.py:76
  348.6 3.4 collective-permute-start.9
  354.4 12.8 %collective-permute-done.9 = bf16[97,3072]{1,0:T(8,128)(2,1)S(1)} collective-permute-done((bf16[97,3072]{1,0:T(8,128)(2,1)S(1)}, bf16[97,3072]{1,0:T(8,128)(2,1)S(1)}, u32[]{:S(2)}, u32[]{:S(2)}) %collective-permute-start.9) | collective-permute-done | bytes 596000 | tf_op jit(solution)/shard_map/ppermute | solution.py:76
  369.4 3.2 collective-permute-done.26
  373.6 12.6 %collective-permute-done.10 = bf16[97,3072]{1,0:T(8,128)(2,1)S(1)} collective-permute-done((bf16[97,3072]{1,0:T(8,128)(2,1)S(1)}, bf16[97,3072]{1,0:T(8,128)(2,1)S(1)}, u32[]{:S(2)}, u32[]{:S(2)}) %collective-permute-start.10) | collective-permute-done | bytes 596000 | tf_op jit(solution)/shard_map/ppermute | solution.py:76
  388.5 9.7 %collective-permute-done.27 = bf16[2,384,768]{2,1,0:T(8,128)(2,1)S(1)} collective-permute-done((bf16[2,384,768]{2,1,0:T(8,128)(2,1)S(1)}, bf16[2,384,768]{2,1,0:T(8,128)(2,1)S(1)}, u32[]{:S(2)}, u32[]{:S(2)}) %collective-permute-start.27) | collective-permute-done | bytes 1179680 | tf_op jit(solution)/shard_map/ppermute | solution.py:76
  398.5 2.6 collective-permute-start.28
  402.3 8.6 %collective-permute-done.11 = bf16[2,97,3072]{2,0,1:T(2,128)(2,1)S(1)} collective-permute-done((bf16[2,97,3072]{2,0,1:T(2,128)(2,1)S(1)}, bf16[2,97,3072]{2,0,1:T(2,128)(2,1)S(1)}, u32[]{:S(2)}, u32[]{:S(2)}) %collective-permute-start.11) | collective-permute-done | bytes 1191968 | tf_op jit(solution)/shard_map/ppermute | solution.py:76
  417.8 3.3 maximum_select_fusion.2
  421.1 5.3 %bitcast_convert_fusion.1 = f32[768,3072]{1,0:T(8,128)} fusion(bf16[2,2,2,96,3072]{4,3,2,1,0:T(8,128)(2,1)S(1)} %maximum_select_fusion.1), kind=kLoop, calls=%fused_computation.45 | loop fusion | flops 2359296 | bytes 14155776 | tf_op jit(solution)/shard_map/convert_element_type | solution.py:298
  426.4 4.8 %bitcast_convert_fusion = f32[3072,768]{1,0:T(8,128)} fusion(bf16[2,2,2,384,768]{4,3,2,1,0:T(8,128)(2,1)S(1)} %maximum_select_fusion.2), kind=kLoop, calls=%fused_computation.42 | loop fusion | flops 2359296 | bytes 14155776 | tf_op jit(solution)/shard_map/convert_element_type | solution.py:297
  436.0 3.9 fusion.220
  (320 shorter events, 100.8 us)
Async XLA Ops:
  0.7 30.0 %copy-start = (bf16[768,768]{1,0:T(8,128)(2,1)S(1)}, bf16[768,768]{1,0:T(8,128)(2,1)}, u32[]{:S(2)}) copy-start(bf16[768,768]{1,0:T(8,128)(2,1)} %param.27) | copy-start | bytes 3538948
  7.6 19.5 %copy-start.10 = (bf16[96,8,8,128]{3,2,1,0:T(8,128)(2,1)}, bf16[96,8,8,128]{3,2,1,0:T(8,128)(2,1)S(1)}, u32[]{:S(2)}) copy-start(bf16[96,8,8,128]{3,2,1,0:T(8,128)(2,1)S(1)} %copy.148) | copy-start | bytes 4718596
  7.8 19.3 %copy-start.33 = (pred[128,128]{0,1:T(8,128)(4,1)}, pred[128,128]{0,1:T(8,128)(4,1)S(1)}, u32[]{:S(2)}) copy-start(pred[128,128]{0,1:T(8,128)(4,1)S(1)} %broadcast_compare_fusion) | copy-start | bytes 49156
  42.1 40.4 %slice-start.6 = ((s8[4718592]{0:T(1024)(128)(4,1)}), s8[4194304]{0:T(1024)(128)(4,1)S(1)}, s32[]{:S(2)}) async-start(s8[4718592]{0:T(1024)(128)(4,1)} %bitcast.308), calls=%async_computation.6 | async-start | bytes 8388608
  42.1 40.4 %slice-start.7 = ((s8[4718592]{0:T(1024)(128)(4,1)}), s8[524288]{0:T(1024)(128)(4,1)S(1)}, s32[]{:S(2)}) async-start(s8[4718592]{0:T(1024)(128)(4,1)} %bitcast.308), calls=%async_computation.7 | async-start | bytes 1048576
  42.1 40.3 %copy-start.19 = (f32[1024,768]{1,0:T(8,128)S(1)}, f32[1024,768]{1,0:T(8,128)}, u32[]{:S(2)}) copy-start(f32[1024,768]{1,0:T(8,128)} %copy-done.18) | copy-start | bytes 9437188
  42.1 38.1 %collective-permute-start = (bf16[16,896]{1,0:T(8,128)(2,1)S(1)}, bf16[16,896]{1,0:T(8,128)(2,1)S(1)}, u32[]{:S(2)}, u32[]{:S(2)}) collective-permute-start(bf16[16,896]{1,0:T(8,128)(2,1)S(1)} %get-tuple-element.61), channel_id=1, source_target_pairs={{0,1},{1,0},{2,3},{3,2},{4,5},{5,4},{6,7},{7,6},{8,9},{9,8},{10,11... | collective-permute-start | bytes 86024 | tf_op jit(solution)/shard_map/ppermute | solution.py:76
  80.2 7.5 %collective-permute-start.1 = (bf16[32,896]{1,0:T(8,128)(2,1)S(1)}, bf16[32,896]{1,0:T(8,128)(2,1)S(1)}, u32[]{:S(2)}, u32[]{:S(2)}) collective-permute-start(bf16[32,896]{1,0:T(8,128)(2,1)S(1)} %pad_maximum_fusion.3), channel_id=1, source_target_pairs={{0,2},{1,3},{2,0},{3,1},{4,6},{5,7},{6,4},{7,5},{8,10},{9,11},{10,... | collective-permute-start | bytes 172040 | tf_op jit(solution)/shard_map/ppermute | solution.py:76
  87.7 19.2 %copy-start.6 = (f32[1024,768]{1,0:T(8,128)}, f32[1024,768]{1,0:T(8,128)S(1)}, u32[]{:S(2)}) copy-start(f32[1024,768]{1,0:T(8,128)S(1)} %get-tuple-element.79) | copy-start | bytes 9437188
  87.7 17.1 %copy-start.23 = (bf16[1,1024,768]{2,1,0:T(8,128)(2,1)S(1)}, bf16[1,1024,768]{2,1,0:T(8,128)(2,1)}, u32[]{:S(2)}) copy-start(bf16[1,1024,768]{2,1,0:T(8,128)(2,1)} %param.37) | copy-start | bytes 4718596
  87.7 4.9 %collective-permute-start.2 = (bf16[64,896]{1,0:T(8,128)(2,1)S(1)}, bf16[64,896]{1,0:T(8,128)(2,1)S(1)}, u32[]{:S(2)}, u32[]{:S(2)}) collective-permute-start(bf16[64,896]{1,0:T(8,128)(2,1)S(1)} %pad_maximum_fusion.2), channel_id=1, source_target_pairs={{0,4},{1,5},{2,6},{3,7},{4,0},{5,1},{6,2},{7,3},{8,12},{9,13},{10,... | collective-permute-start | bytes 344072 | tf_op jit(solution)/shard_map/ppermute | solution.py:76
  92.6 11.6 %collective-permute-start.3 = (bf16[128,896]{1,0:T(8,128)(2,1)S(1)}, bf16[128,896]{1,0:T(8,128)(2,1)S(1)}, u32[]{:S(2)}, u32[]{:S(2)}) collective-permute-start(bf16[128,896]{1,0:T(8,128)(2,1)S(1)} %pad_maximum_fusion.1), channel_id=1, source_target_pairs={{0,8},{1,9},{2,10},{3,11},{4,12},{5,13},{6,14},{7,15},{8,0},{9,1},... | collective-permute-start | bytes 688136 | tf_op jit(solution)/shard_map/ppermute | solution.py:76
  104.2 2.8 collective-permute-start.4
  117.9 18.5 %slice-start.10 = ((s8[4718592]{0:T(1024)(128)(4,1)}), s8[4194304]{0:T(1024)(128)(4,1)S(1)}, s32[]{:S(2)}) async-start(s8[4718592]{0:T(1024)(128)(4,1)} %bitcast.312), calls=%async_computation.10 | async-start | bytes 8388608
  121.4 15.0 %copy-start.21 = (f32[1024,768]{1,0:T(8,128)}, f32[1024,768]{1,0:T(8,128)S(1)}, u32[]{:S(2)}) copy-start(f32[1024,768]{1,0:T(8,128)S(1)} %get-tuple-element.39) | copy-start | bytes 9437188
  122.0 14.5 %copy-start.5 = (f32[1024,768]{1,0:T(8,128)S(1)}, f32[1024,768]{1,0:T(8,128)}, u32[]{:S(2)}) copy-start(f32[1024,768]{1,0:T(8,128)} %copy-done.4) | copy-start | bytes 9437188
  122.0 14.5 %slice-start.11 = ((s8[4718592]{0:T(1024)(128)(4,1)}), s8[524288]{0:T(1024)(128)(4,1)S(1)}, s32[]{:S(2)}) async-start(s8[4718592]{0:T(1024)(128)(4,1)} %bitcast.312), calls=%async_computation.11 | async-start | bytes 1048576
  122.0 14.5 %copy-start.37 = (f32[1024]{0:T(1024)S(1)}, f32[1024]{0:T(1024)}, u32[]{:S(2)}) copy-start(f32[1024]{0:T(1024)} %copy-done.36) | copy-start | bytes 12292
  122.0 14.5 %copy-start.40 = (f32[1024]{0:T(1024)S(1)}, f32[1024]{0:T(1024)}, u32[]{:S(2)}) copy-start(f32[1024]{0:T(1024)} %copy-done.39) | copy-start | bytes 12292
  122.0 14.5 %copy-start.42 = (f32[768]{0:T(1024)S(1)}, f32[768]{0:T(1024)}, u32[]{:S(2)}) copy-start(f32[768]{0:T(1024)} %param.29) | copy-start | bytes 9220
  170.1 10.3 %slice-start.12 = ((s8[6291456]{0:T(1024)(128)(4,1)}), s8[4194304]{0:T(1024)(128)(4,1)S(1)}, s32[]{:S(2)}) async-start(s8[6291456]{0:T(1024)(128)(4,1)} %bitcast.328), calls=%async_computation.12 | async-start | bytes 8388608
  172.0 8.5 %slice-start.13 = ((s8[6291456]{0:T(1024)(128)(4,1)}), s8[2097152]{0:T(1024)(128)(4,1)S(1)}, s32[]{:S(2)}) async-start(s8[6291456]{0:T(1024)(128)(4,1)} %bitcast.328), calls=%async_computation.13 | async-start | bytes 4194304
  180.5 15.2 %copy-start.17 = (bf16[768,3072]{1,0:T(8,128)(2,1)}, bf16[768,3072]{1,0:T(8,128)(2,1)S(1)}, u32[]{:S(2)}) copy-start(bf16[768,3072]{1,0:T(8,128)(2,1)S(1)} %convolution_convert_fusion.1) | copy-start | bytes 14155780
  197.3 27.6 %collective-permute-start.13 = (bf16[2,2,96,3072]{3,2,1,0:T(8,128)(2,1)}, bf16[2,2,96,3072]{3,2,1,0:T(8,128)(2,1)}, u32[]{:S(2)}, u32[]{:S(2)}) collective-permute-start(bf16[2,2,96,3072]{3,2,1,0:T(8,128)(2,1)} %dynamic-slice_bitcast_fusion.1), channel_id=1, source_target_pairs={{0,16},{1,17},{2,18},{3,19},{4,20},{5,21},{6,22},{7,23},{8,24},{9,... | collective-permute-start | bytes 7077896 | tf_op jit(solution)/shard_map/ppermute | solution.py:76
  212.2 15.6 %collective-permute-start.21 = (bf16[2,2,384,768]{3,2,1,0:T(8,128)(2,1)}, bf16[2,2,384,768]{3,2,1,0:T(8,128)(2,1)}, u32[]{:S(2)}, u32[]{:S(2)}) collective-permute-start(bf16[2,2,384,768]{3,2,1,0:T(8,128)(2,1)} %dynamic-slice_bitcast_fusion), channel_id=1, source_target_pairs={{0,16},{1,17},{2,18},{3,19},{4,20},{5,21},{6,22},{7,23},{8,24},{9,... | collective-permute-start | bytes 7077896 | tf_op jit(solution)/shard_map/ppermute | solution.py:76
  217.9 14.2 %collective-permute-start.5 = (bf16[2,2,97,3072]{3,1,2,0:T(2,128)(2,1)S(1)}, bf16[2,2,97,3072]{3,1,2,0:T(2,128)(2,1)S(1)}, u32[]{:S(2)}, u32[]{:S(2)}) collective-permute-start(bf16[2,2,97,3072]{3,1,2,0:T(2,128)(2,1)S(1)} %bitcast.315), channel_id=1, source_target_pairs={{0,16},{1,17},{2,18},{3,19},{4,20},{5,21},{6,22},{7,23},{8,24},{9,... | collective-permute-start | bytes 7151624 | tf_op jit(solution)/shard_map/ppermute | solution.py:76
  218.5 9.3 %slice-start.2 = ((s8[4718592]{0:T(1024)(128)(4,1)}), s8[4194304]{0:T(1024)(128)(4,1)S(1)}, s32[]{:S(2)}) async-start(s8[4718592]{0:T(1024)(128)(4,1)} %bitcast.301), calls=%async_computation.2 | async-start | bytes 8388608
  227.6 16.3 %collective-permute-start.14 = (bf16[2,96,3072]{2,1,0:T(8,128)(2,1)S(1)}, bf16[2,96,3072]{2,1,0:T(8,128)(2,1)S(1)}, u32[]{:S(2)}, u32[]{:S(2)}) collective-permute-start(bf16[2,96,3072]{2,1,0:T(8,128)(2,1)S(1)} %dynamic-slice_bitcast_fusion.3), channel_id=1, source_target_pairs={{0,1},{1,0},{2,3},{3,2},{4,5},{5,4},{6,7},{7,6},{8,9},{9,8},{10,11... | collective-permute-start | bytes 3538952 | tf_op jit(solution)/shard_map/ppermute | solution.py:76
  230.1 32.7 %collective-permute-start.22 = (bf16[2,384,768]{2,1,0:T(8,128)(2,1)S(1)}, bf16[2,384,768]{2,1,0:T(8,128)(2,1)S(1)}, u32[]{:S(2)}, u32[]{:S(2)}) collective-permute-start(bf16[2,384,768]{2,1,0:T(8,128)(2,1)S(1)} %dynamic-slice_bitcast_fusion.2), channel_id=1, source_target_pairs={{0,1},{1,0},{2,3},{3,2},{4,5},{5,4},{6,7},{7,6},{8,9},{9,8},{10,11... | collective-permute-start | bytes 3538952 | tf_op jit(solution)/shard_map/ppermute | solution.py:76
  234.4 47.5 %collective-permute-start.6 = (bf16[2,97,3072]{2,0,1:T(2,128)(2,1)S(1)}, bf16[2,97,3072]{2,0,1:T(2,128)(2,1)S(1)}, u32[]{:S(2)}, u32[]{:S(2)}) collective-permute-start(bf16[2,97,3072]{2,0,1:T(2,128)(2,1)S(1)} %bitcast.325), channel_id=1, source_target_pairs={{0,1},{1,0},{2,3},{3,2},{4,5},{5,4},{6,7},{7,6},{8,9},{9,8},{10,11... | collective-permute-start | bytes 3575816 | tf_op jit(solution)/shard_map/ppermute | solution.py:76
  244.7 38.3 %collective-permute-start.15 = (bf16[96,3072]{1,0:T(8,128)(2,1)S(1)}, bf16[96,3072]{1,0:T(8,128)(2,1)S(1)}, u32[]{:S(2)}, u32[]{:S(2)}) collective-permute-start(bf16[96,3072]{1,0:T(8,128)(2,1)S(1)} %dynamic-slice_bitcast_fusion.6), channel_id=1, source_target_pairs={{0,2},{1,3},{2,0},{3,1},{4,6},{5,7},{6,4},{7,5},{8,10},{9,11},{10,... | collective-permute-start | bytes 1769480 | tf_op jit(solution)/shard_map/ppermute | solution.py:76
  263.2 20.7 %collective-permute-start.23 = (bf16[384,768]{1,0:T(8,128)(2,1)S(1)}, bf16[384,768]{1,0:T(8,128)(2,1)S(1)}, u32[]{:S(2)}, u32[]{:S(2)}) collective-permute-start(bf16[384,768]{1,0:T(8,128)(2,1)S(1)} %dynamic-slice_bitcast_fusion.5), channel_id=1, source_target_pairs={{0,2},{1,3},{2,0},{3,1},{4,6},{5,7},{6,4},{7,5},{8,10},{9,11},{10,... | collective-permute-start | bytes 1769480 | tf_op jit(solution)/shard_map/ppermute | solution.py:76
  282.4 10.5 %collective-permute-start.7 = (bf16[97,3072]{1,0:T(8,128)(2,1)S(1)}, bf16[97,3072]{1,0:T(8,128)(2,1)S(1)}, u32[]{:S(2)}, u32[]{:S(2)}) collective-permute-start(bf16[97,3072]{1,0:T(8,128)(2,1)S(1)} %dynamic-slice_bitcast_fusion.4), channel_id=1, source_target_pairs={{0,2},{1,3},{2,0},{3,1},{4,6},{5,7},{6,4},{7,5},{8,10},{9,11},{10,... | collective-permute-start | bytes 1787912 | tf_op jit(solution)/shard_map/ppermute | solution.py:76
  283.1 14.6 %collective-permute-start.16 = (bf16[96,3072]{1,0:T(8,128)(2,1)S(1)}, bf16[96,3072]{1,0:T(8,128)(2,1)S(1)}, u32[]{:S(2)}, u32[]{:S(2)}) collective-permute-start(bf16[96,3072]{1,0:T(8,128)(2,1)S(1)} %fusion.106), channel_id=1, source_target_pairs={{0,4},{1,5},{2,6},{3,7},{4,0},{5,1},{6,2},{7,3},{8,12},{9,13},{10,... | collective-permute-start | bytes 1769480 | tf_op jit(solution)/shard_map/ppermute | solution.py:76
  284.1 34.7 %collective-permute-start.24 = (bf16[384,768]{1,0:T(8,128)(2,1)S(1)}, bf16[384,768]{1,0:T(8,128)(2,1)S(1)}, u32[]{:S(2)}, u32[]{:S(2)}) collective-permute-start(bf16[384,768]{1,0:T(8,128)(2,1)S(1)} %fusion.105), channel_id=1, source_target_pairs={{0,4},{1,5},{2,6},{3,7},{4,0},{5,1},{6,2},{7,3},{8,12},{9,13},{10,... | collective-permute-start | bytes 1769480 | tf_op jit(solution)/shard_map/ppermute | solution.py:76
  293.0 55.4 %collective-permute-start.8 = (bf16[97,3072]{1,0:T(8,128)(2,1)S(1)}, bf16[97,3072]{1,0:T(8,128)(2,1)S(1)}, u32[]{:S(2)}, u32[]{:S(2)}) collective-permute-start(bf16[97,3072]{1,0:T(8,128)(2,1)S(1)} %fusion.104), channel_id=1, source_target_pairs={{0,4},{1,5},{2,6},{3,7},{4,0},{5,1},{6,2},{7,3},{8,12},{9,13},{10,... | collective-permute-start | bytes 1787912 | tf_op jit(solution)/shard_map/ppermute | solution.py:76
  297.8 54.1 %collective-permute-start.17 = (bf16[96,3072]{1,0:T(8,128)(2,1)S(1)}, bf16[96,3072]{1,0:T(8,128)(2,1)S(1)}, u32[]{:S(2)}, u32[]{:S(2)}) collective-permute-start(bf16[96,3072]{1,0:T(8,128)(2,1)S(1)} %add_convert_fusion.8), channel_id=1, source_target_pairs={{0,8},{1,9},{2,10},{3,11},{4,12},{5,13},{6,14},{7,15},{8,0},{9,1},... | collective-permute-start | bytes 1769480 | tf_op jit(solution)/shard_map/ppermute | solution.py:76
  318.9 34.8 %collective-permute-start.25 = (bf16[384,768]{1,0:T(8,128)(2,1)S(1)}, bf16[384,768]{1,0:T(8,128)(2,1)S(1)}, u32[]{:S(2)}, u32[]{:S(2)}) collective-permute-start(bf16[384,768]{1,0:T(8,128)(2,1)S(1)} %add_convert_fusion.6), channel_id=1, source_target_pairs={{0,8},{1,9},{2,10},{3,11},{4,12},{5,13},{6,14},{7,15},{8,0},{9,1},... | collective-permute-start | bytes 1769480 | tf_op jit(solution)/shard_map/ppermute | solution.py:76
  348.6 18.7 %collective-permute-start.9 = (bf16[97,3072]{1,0:T(8,128)(2,1)S(1)}, bf16[97,3072]{1,0:T(8,128)(2,1)S(1)}, u32[]{:S(2)}, u32[]{:S(2)}) collective-permute-start(bf16[97,3072]{1,0:T(8,128)(2,1)S(1)} %add_convert_fusion.4), channel_id=1, source_target_pairs={{0,8},{1,9},{2,10},{3,11},{4,12},{5,13},{6,14},{7,15},{8,0},{9,1},... | collective-permute-start | bytes 1787912 | tf_op jit(solution)/shard_map/ppermute | solution.py:76
  352.1 16.9 %collective-permute-start.18 = (bf16[96,3072]{1,0:T(8,128)(2,1)S(1)}, bf16[96,3072]{1,0:T(8,128)(2,1)S(1)}, u32[]{:S(2)}, u32[]{:S(2)}) collective-permute-start(bf16[96,3072]{1,0:T(8,128)(2,1)S(1)} %add_convert_fusion.7), channel_id=1, source_target_pairs={{0,2},{1,3},{2,0},{3,1},{4,6},{5,7},{6,4},{7,5},{8,10},{9,11},{10,... | collective-permute-start | bytes 1769480 | tf_op jit(solution)/shard_map/ppermute | solution.py:76
  353.9 18.7 %collective-permute-start.26 = (bf16[384,768]{1,0:T(8,128)(2,1)S(1)}, bf16[384,768]{1,0:T(8,128)(2,1)S(1)}, u32[]{:S(2)}, u32[]{:S(2)}) collective-permute-start(bf16[384,768]{1,0:T(8,128)(2,1)S(1)} %add_convert_fusion.5), channel_id=1, source_target_pairs={{0,2},{1,3},{2,0},{3,1},{4,6},{5,7},{6,4},{7,5},{8,10},{9,11},{10,... | collective-permute-start | bytes 1769480 | tf_op jit(solution)/shard_map/ppermute | solution.py:76
  367.4 18.8 %collective-permute-start.10 = (bf16[97,3072]{1,0:T(8,128)(2,1)S(1)}, bf16[97,3072]{1,0:T(8,128)(2,1)S(1)}, u32[]{:S(2)}, u32[]{:S(2)}) collective-permute-start(bf16[97,3072]{1,0:T(8,128)(2,1)S(1)} %add_convert_fusion.3), channel_id=1, source_target_pairs={{0,2},{1,3},{2,0},{3,1},{4,6},{5,7},{6,4},{7,5},{8,10},{9,11},{10,... | collective-permute-start | bytes 1787912 | tf_op jit(solution)/shard_map/ppermute | solution.py:76
  369.2 18.8 %collective-permute-start.19 = (bf16[2,96,3072]{2,1,0:T(8,128)(2,1)S(1)}, bf16[2,96,3072]{2,1,0:T(8,128)(2,1)S(1)}, u32[]{:S(2)}, u32[]{:S(2)}) collective-permute-start(bf16[2,96,3072]{2,1,0:T(8,128)(2,1)S(1)} %maximum_select_fusion.12), channel_id=1, source_target_pairs={{0,1},{1,0},{2,3},{3,2},{4,5},{5,4},{6,7},{7,6},{8,9},{9,8},{10,11... | collective-permute-start | bytes 3538952 | tf_op jit(solution)/shard_map/ppermute | solution.py:76
  372.7 25.4 %collective-permute-start.27 = (bf16[2,384,768]{2,1,0:T(8,128)(2,1)S(1)}, bf16[2,384,768]{2,1,0:T(8,128)(2,1)S(1)}, u32[]{:S(2)}, u32[]{:S(2)}) collective-permute-start(bf16[2,384,768]{2,1,0:T(8,128)(2,1)S(1)} %maximum_select_fusion.14), channel_id=1, source_target_pairs={{0,1},{1,0},{2,3},{3,2},{4,5},{5,4},{6,7},{7,6},{8,9},{9,8},{10,11... | collective-permute-start | bytes 3538952 | tf_op jit(solution)/shard_map/ppermute | solution.py:76
  387.7 23.2 %collective-permute-start.11 = (bf16[2,97,3072]{2,0,1:T(2,128)(2,1)S(1)}, bf16[2,97,3072]{2,0,1:T(2,128)(2,1)S(1)}, u32[]{:S(2)}, u32[]{:S(2)}) collective-permute-start(bf16[2,97,3072]{2,0,1:T(2,128)(2,1)S(1)} %copy.137), channel_id=1, source_target_pairs={{0,1},{1,0},{2,3},{3,2},{4,5},{5,4},{6,7},{7,6},{8,9},{9,8},{10,11... | collective-permute-start | bytes 3575816 | tf_op jit(solution)/shard_map/ppermute | solution.py:76
  388.3 28.7 %collective-permute-start.20 = (bf16[2,2,96,3072]{3,2,1,0:T(8,128)(2,1)S(1)}, bf16[2,2,96,3072]{3,2,1,0:T(8,128)(2,1)S(1)}, u32[]{:S(2)}, u32[]{:S(2)}) collective-permute-start(bf16[2,2,96,3072]{3,2,1,0:T(8,128)(2,1)S(1)} %maximum_select_fusion.6), channel_id=1, source_target_pairs={{0,16},{1,17},{2,18},{3,19},{4,20},{5,21},{6,22},{7,23},{8,24},{9,... | collective-permute-start | bytes 7077896 | tf_op jit(solution)/shard_map/ppermute | solution.py:76
  398.5 19.3 %collective-permute-start.28 = (bf16[2,2,384,768]{3,2,1,0:T(8,128)(2,1)S(1)}, bf16[2,2,384,768]{3,2,1,0:T(8,128)(2,1)}, u32[]{:S(2)}, u32[]{:S(2)}) collective-permute-start(bf16[2,2,384,768]{3,2,1,0:T(8,128)(2,1)S(1)} %maximum_select_fusion.8), channel_id=1, source_target_pairs={{0,16},{1,17},{2,18},{3,19},{4,20},{5,21},{6,22},{7,23},{8,24},{9,... | collective-permute-start | bytes 7077896 | tf_op jit(solution)/shard_map/ppermute | solution.py:76
  414.2 16.9 %collective-permute-start.12 = (bf16[2,2,97,3072]{3,1,2,0:T(2,128)(2,1)S(1)}, bf16[2,2,97,3072]{3,1,2,0:T(2,128)(2,1)S(1)}, u32[]{:S(2)}, u32[]{:S(2)}) collective-permute-start(bf16[2,2,97,3072]{3,1,2,0:T(2,128)(2,1)S(1)} %copy.140), channel_id=1, source_target_pairs={{0,16},{1,17},{2,18},{3,19},{4,20},{5,21},{6,22},{7,23},{8,24},{9,... | collective-permute-start | bytes 7151624 | tf_op jit(solution)/shard_map/ppermute | solution.py:76
  (52 other events, 176.7 us)
